TPU v7x, 32 devices: a whole 2x2x4 slice. The times are simulated.
32 devices in a mesh: seq: 2 (over core), hid: 16 (over z, y, x).
Axes of the slice: x: 2, y: 2, z: 4, core: 2. Of those that a mesh axis runs over, the one named last changes fastest.
Arguments:
- inputs: bfloat16 [2, 768, 2048], P('seq', 'hid'), may hold values from -6 to 6
- cotangent: bfloat16 [2, 768, 2048], P('seq', 'hid'), may hold values from -6 to 6
- lengths: int32 [12], replicated, may hold values from 1 to 1024, 1536 in all
- first_gain: float32 [2048], replicated, may hold values from 0.25 to 1.75
- q_weight: bfloat16 [2048, 2048], P(('seq', 'hid')), may hold values from -0.125 to 0.125
- f_weight: bfloat16 [2048, 2048], P(('seq', 'hid')), may hold values from -0.125 to 0.125
- i_weight: bfloat16 [2048, 2048], P(('seq', 'hid')), may hold values from -0.125 to 0.125
- o_weight: bfloat16 [2048, 2048], P(('seq', 'hid')), may hold values from -0.125 to 0.125
- group_gain: float32 [128], replicated, may hold values from 0.25 to 1.75
- gap_log: float32 [2048], replicated, may hold values from -11.5 to -3.5
- second_gain: float32 [2048], replicated, may hold values from 0.25 to 1.75
- gate_weight: bfloat16 [2048, 5632], P(('seq', 'hid')), may hold values from -0.125 to 0.125
- up_weight: bfloat16 [2048, 5632], P(('seq', 'hid')), may hold values from -0.125 to 0.125
- down_weight: bfloat16 [2048, 5632], P(('seq', 'hid')), may hold values from -0.078125 to 0.078125
Outputs:
- output: bfloat16 [2, 768, 2048], P('seq', 'hid')
- input_grad: float32 [2, 768, 2048], P('seq', 'hid')
- first_grad: float32 [2048], replicated
- q_grad: float32 [2048, 2048], P(('seq', 'hid'))
- f_grad: float32 [2048, 2048], P(('seq', 'hid'))
- i_grad: float32 [2048, 2048], P(('seq', 'hid'))
- o_grad: float32 [2048, 2048], P(('seq', 'hid'))
- group_grad: float32 [128], replicated
- gap_grad: float32 [2048], replicated
- second_grad: float32 [2048], replicated
- gate_grad: float32 [2048, 5632], P(('seq', 'hid'))
- up_grad: float32 [2048, 5632], P(('seq', 'hid'))
- down_grad: float32 [2048, 5632], P(('seq', 'hid'))
Inputs may be any that keep to these rules, and one draw needn't show every extreme that they name: The 12 documents fill the 1536 positions in order; the lengths sum to 1536 and the largest is exactly 1024.
All inputs are finite; a program needn't handle non-finite values.
Results may differ from a plain program's by a relative error of at most 0.015.
Values may be sent and summed in bfloat16 or wider, within the bound.
A program may use at most 320 MiB of HBM per device.

v0:
```python
import functools

import jax
import jax.numpy as jnp
from jax import lax
from jax.experimental import pallas as pl
from jax.experimental.pallas import tpu as pltpu
from jax.sharding import PartitionSpec as P

H = 16
SPAN = 128


EPS = 1e-06
HIGH_PRECISION = lax.Precision.HIGHEST


def from_behind(block, axis, distance):
    devices = range(lax.axis_size(axis))
    route = [(i - distance, i) for i in devices if i - distance in devices]
    return lax.ppermute(block, axis, route)


def normed(entries, gain_vec):
    factor = lax.rsqrt(jnp.mean(entries * entries, axis=-1, keepdims=True) + EPS)
    return entries * factor * gain_vec


def gates(q_part, f_part, gap_piece):
    key_gate = jnp.exp(gap_piece) * jax.nn.sigmoid(-f_part)
    return (jax.nn.silu(q_part), key_gate, jnp.log1p(-key_gate))


def doc_starts(lengths):
    count = lengths.shape[0]
    earlier = lax.broadcasted_iota(jnp.int32, (count, count), 0) > lax.broadcasted_iota(
        jnp.int32, (count, count), 1
    )
    return jnp.sum(jnp.where(earlier, lengths[None, :], 0), axis=1)


def running_sum(rows):
    extent = rows.shape[-2]
    lower = (
        lax.broadcasted_iota(jnp.int32, (extent, extent), 0)
        >= lax.broadcasted_iota(jnp.int32, (extent, extent), 1)
    ).astype(jnp.float32)
    return jnp.einsum("ts,...sk->...tk", lower, rows, precision=HIGH_PRECISION)


def doc_ids(lengths, positions):
    starts = doc_starts(lengths)
    covered = (starts[None, :] <= positions[:, None]).astype(jnp.int32)
    return jnp.sum(covered, axis=1) - 1


def span_step(memory_state, pieces):
    queries, key_gate, value_rows, log_decay, documents, before = pieces
    cumulative = running_sum(log_decay)
    query_decayed = queries * jnp.exp(cumulative)
    k_grown = key_gate * jnp.exp(-cumulative)
    extent = documents.shape[0]
    row_ids = lax.broadcasted_iota(jnp.int32, (extent, extent), 0)
    col_ids = lax.broadcasted_iota(jnp.int32, (extent, extent), 1)
    same_doc = jnp.logical_and(documents[:, None] == documents[None, :], row_ids >= col_ids).astype(
        jnp.float32
    )
    scores = (
        jnp.einsum("hck,hsk->hcs", query_decayed, k_grown, precision=HIGH_PRECISION)
        * same_doc[None]
    )
    within_block = jnp.einsum("hcs,hsv->hcv", scores, value_rows, precision=HIGH_PRECISION)
    carried_state = (documents == before).astype(jnp.float32)[None, :, None]
    output_rows = within_block + carried_state * jnp.einsum(
        "awn,ani->awi", query_decayed, memory_state, precision=HIGH_PRECISION
    )
    last_cum = cumulative[:, -1:, :]
    keep_mask = (documents == documents[-1]).astype(jnp.float32)[None, :, None]
    tail_key_rows = jnp.exp(last_cum - cumulative) * key_gate * keep_mask
    whole_block = (documents[-1] == before).astype(jnp.float32)
    fresh_state = jnp.einsum("wfx,wfg->wxg", tail_key_rows, value_rows, precision=HIGH_PRECISION)
    memory_state = jnp.exp(last_cum[:, 0, :])[:, :, None] * whole_block * memory_state + fresh_state
    return (memory_state, output_rows)


def recur(queries, key_gate, value_rows, log_decay, documents, before, memory_state):
    head_count, extent, columns = queries.shape
    span_count = extent // SPAN

    def by_span(tensor):
        return jnp.swapaxes(tensor.reshape(head_count, span_count, SPAN, tensor.shape[-1]), 0, 1)

    doc_rows = documents.reshape(span_count, SPAN)
    befores = jnp.concatenate([jnp.reshape(before, (1,)), doc_rows[:-1, -1]])
    memory_state, span_out = lax.scan(
        jax.checkpoint(span_step),
        memory_state,
        (
            by_span(queries),
            by_span(key_gate),
            by_span(value_rows),
            by_span(log_decay),
            doc_rows,
            befores,
        ),
    )
    return (
        jnp.swapaxes(span_out, 0, 1).reshape(head_count, extent, value_rows.shape[-1]),
        memory_state,
    )


def spread_cols(weight, copies):
    row_count = weight.shape[0]
    shaped = weight.reshape(row_count, 1, H, weight.shape[1] // H)
    return jnp.broadcast_to(shaped, (row_count, copies, H, shaped.shape[3])).reshape(
        row_count, copies * weight.shape[1]
    )


def fold_copies(received, copies):
    row_count = received.shape[0]
    return jnp.sum(received.reshape(row_count, copies, received.shape[1] // copies), axis=1)


def fan_rows(local_rows):
    blocks_here, row_count, columns = local_rows.shape
    return jnp.broadcast_to(local_rows[:, None], (blocks_here, H, row_count, columns)).reshape(
        blocks_here * H * row_count, columns
    )


def sum_heads(received, blocks_here):
    total_rows, columns = received.shape
    return jnp.sum(
        received.reshape(blocks_here, H, total_rows // (blocks_here * H), columns), axis=1
    )


def times_t(left_mat, right_mat):
    return lax.dot_general(
        left_mat, right_mat, (((1,), (1,)), ((), ())), preferred_element_type=jnp.float32
    )


def outer_sum(left_mat, right_mat):
    return lax.dot_general(
        left_mat, right_mat, (((0,), (0,)), ((), ())), preferred_element_type=jnp.float32
    )


def outer_high(left_mat, right_mat):
    return lax.dot_general(
        left_mat,
        right_mat,
        (((0,), (0,)), ((), ())),
        precision=HIGH_PRECISION,
        preferred_element_type=jnp.float32,
    )


def wide_body(
    inputs,
    cotangent,
    lengths,
    first_gain,
    q_weight,
    f_weight,
    i_weight,
    o_weight,
    group_gain,
    gap_log,
    second_gain,
    gate_weight,
    up_weight,
    down_weight,
):
    hid_size = lax.axis_size("hid")
    per_seq = hid_size // H
    block_total = lax.axis_size("seq") * per_seq
    hid_place = lax.axis_index("hid")
    head_id = hid_place % H
    block_id = lax.axis_index("seq") * per_seq + hid_place // H
    model = inputs.shape[2]
    head_width = model // H
    block_len = hid_size * inputs.shape[1]
    entries = inputs.astype(jnp.float32)
    q_block, f_block, i_block, o_block, gate_block, up_block, down_block = (
        lax.all_to_all(
            spread_cols(q_weight, block_total),
            ("seq", "hid"),
            split_axis=1,
            concat_axis=0,
            tiled=True,
        ),
        lax.all_to_all(
            spread_cols(f_weight, block_total),
            ("seq", "hid"),
            split_axis=1,
            concat_axis=0,
            tiled=True,
        ),
        lax.all_to_all(
            spread_cols(i_weight, block_total),
            ("seq", "hid"),
            split_axis=1,
            concat_axis=0,
            tiled=True,
        ),
        lax.all_to_all(
            spread_cols(o_weight, block_total),
            ("seq", "hid"),
            split_axis=1,
            concat_axis=0,
            tiled=True,
        ),
        lax.all_to_all(
            spread_cols(gate_weight, block_total),
            ("seq", "hid"),
            split_axis=1,
            concat_axis=0,
            tiled=True,
        ),
        lax.all_to_all(
            spread_cols(up_weight, block_total),
            ("seq", "hid"),
            split_axis=1,
            concat_axis=0,
            tiled=True,
        ),
        lax.all_to_all(
            spread_cols(down_weight, block_total),
            ("seq", "hid"),
            split_axis=1,
            concat_axis=0,
            tiled=True,
        ),
    )
    positions = block_id * block_len + lax.iota(jnp.int32, block_len)
    documents = doc_ids(lengths, positions)
    before = doc_ids(lengths, jnp.reshape(block_id * block_len - 1, (1,)))[0]
    first_norm, first_back = jax.vjp(normed, entries, first_gain)
    first_low = first_norm.astype(jnp.bfloat16)
    first_rows = lax.all_to_all(fan_rows(first_low), "hid", split_axis=0, concat_axis=0, tiled=True)
    q_lin = jnp.dot(first_rows, q_block, preferred_element_type=jnp.float32)
    f_lin = jnp.dot(first_rows, f_block, preferred_element_type=jnp.float32)
    i_lin = jnp.dot(first_rows, i_block, preferred_element_type=jnp.float32)
    gap_part = lax.dynamic_slice_in_dim(gap_log, head_id * head_width, head_width)
    queries, key_gate, log_decay = gates(q_lin, f_lin, gap_part)
    cumulative = running_sum(log_decay)
    last_cum = cumulative[-1]
    tail_key_rows = (
        jnp.exp(last_cum[None, :] - cumulative)
        * key_gate
        * (documents == documents[-1]).astype(jnp.float32)[:, None]
    )
    local_state = outer_high(tail_key_rows, i_lin)
    decay = jnp.exp(last_cum) * (documents[-1] == before).astype(jnp.float32)
    state_in = jnp.zeros_like(local_state)
    for number in range(block_total - 1):
        state_out = decay[:, None] * state_in + local_state
        state_in = from_behind(state_out.astype(jnp.bfloat16), ("seq", "hid"), H).astype(
            state_out.dtype
        )

    def core(q_part, f_part, i_part, gap_piece):
        queries_in, keys_in, logs_in = gates(q_part, f_part, gap_piece)
        mixed_all, memory_state = recur(
            queries_in[None],
            keys_in[None],
            i_part[None],
            logs_in[None],
            documents,
            before,
            state_in[None],
        )
        return (mixed_all[0], memory_state[0])

    (mixed_out, _), core_back = jax.vjp(core, q_lin, f_lin, i_lin, gap_part)
    head_normed, norm_back = jax.vjp(normed, mixed_out, group_gain)
    head_low = head_normed.astype(jnp.bfloat16)
    mix_out = sum_heads(
        lax.all_to_all(
            times_t(head_low, o_block).astype(jnp.bfloat16),
            "hid",
            split_axis=0,
            concat_axis=0,
            tiled=True,
        ).astype(jnp.float32),
        per_seq,
    )
    middle = entries + mix_out
    second_norm, second_back = jax.vjp(normed, middle, second_gain)
    second_low = second_norm.astype(jnp.bfloat16)
    second_rows, cot_rows = (
        lax.all_to_all(fan_rows(second_low), "hid", split_axis=0, concat_axis=0, tiled=True),
        lax.all_to_all(fan_rows(cotangent), "hid", split_axis=0, concat_axis=0, tiled=True),
    )
    gate_lin = jnp.dot(second_rows, gate_block, preferred_element_type=jnp.float32)
    up_lin = jnp.dot(second_rows, up_block, preferred_element_type=jnp.float32)
    hidden = (jax.nn.silu(gate_lin) * up_lin).astype(jnp.bfloat16)
    glu_out = sum_heads(
        lax.all_to_all(
            times_t(hidden, down_block).astype(jnp.bfloat16),
            "hid",
            split_axis=0,
            concat_axis=0,
            tiled=True,
        ).astype(jnp.float32),
        per_seq,
    )
    output = (middle + glu_out).astype(jnp.bfloat16)
    down_part = outer_sum(cot_rows, hidden)
    hidden_grad = jnp.dot(cot_rows, down_block, preferred_element_type=jnp.float32)
    gate_sig = jax.nn.sigmoid(gate_lin)
    gate_low = (hidden_grad * up_lin * gate_sig * (1.0 + gate_lin * (1.0 - gate_sig))).astype(
        jnp.bfloat16
    )
    up_low = (hidden_grad * gate_lin * gate_sig).astype(jnp.bfloat16)
    gate_part = outer_sum(second_rows, gate_low)
    up_part = outer_sum(second_rows, up_low)
    second_sum = lax.all_to_all(
        (times_t(gate_low, gate_block) + times_t(up_low, up_block)).astype(jnp.bfloat16),
        "hid",
        split_axis=0,
        concat_axis=0,
        tiled=True,
    ).astype(jnp.float32)
    middle_part, second_part = second_back(sum_heads(second_sum, per_seq))
    middle_grad = cotangent.astype(jnp.float32) + middle_part
    mix_grad = middle_grad.astype(jnp.bfloat16)
    mix_rows = lax.all_to_all(fan_rows(mix_grad), "hid", split_axis=0, concat_axis=0, tiled=True)
    normed_grad = jnp.dot(mix_rows, o_block, preferred_element_type=jnp.float32)
    o_part = outer_sum(mix_rows, head_low)
    mixed_grad, group_part = norm_back(normed_grad)
    carried_state = (documents == before).astype(jnp.float32)[:, None]
    grad_local = outer_high(queries * jnp.exp(cumulative) * carried_state, mixed_grad)
    state_grad = jnp.zeros_like(grad_local)
    for number in range(block_total - 1):
        grad_in = decay[:, None] * state_grad + grad_local
        state_grad = from_behind(grad_in.astype(jnp.bfloat16), ("seq", "hid"), -H).astype(
            grad_in.dtype
        )
    q_grad_lin, f_grad_lin, i_grad_lin, gap_piece_grad = core_back((mixed_grad, state_grad))
    q_low = q_grad_lin.astype(jnp.bfloat16)
    f_low = f_grad_lin.astype(jnp.bfloat16)
    i_low = i_grad_lin.astype(jnp.bfloat16)
    q_part = outer_sum(first_rows, q_low)
    f_part = outer_sum(first_rows, f_low)
    i_part = outer_sum(first_rows, i_low)
    first_sum = lax.all_to_all(
        (times_t(q_low, q_block) + times_t(f_low, f_block) + times_t(i_low, i_block)).astype(
            jnp.bfloat16
        ),
        "hid",
        split_axis=0,
        concat_axis=0,
        tiled=True,
    ).astype(jnp.float32)
    entry_part, first_part = first_back(sum_heads(first_sum, per_seq))
    input_grad = middle_grad + entry_part
    q_back, f_back, i_back, o_back, gate_back, up_back, down_back = (
        lax.all_to_all(
            q_part.astype(jnp.bfloat16), ("seq", "hid"), split_axis=0, concat_axis=1, tiled=True
        ).astype(q_part.dtype),
        lax.all_to_all(
            f_part.astype(jnp.bfloat16), ("seq", "hid"), split_axis=0, concat_axis=1, tiled=True
        ).astype(f_part.dtype),
        lax.all_to_all(
            i_part.astype(jnp.bfloat16), ("seq", "hid"), split_axis=0, concat_axis=1, tiled=True
        ).astype(i_part.dtype),
        lax.all_to_all(
            o_part.astype(jnp.bfloat16), ("seq", "hid"), split_axis=0, concat_axis=1, tiled=True
        ).astype(o_part.dtype),
        lax.all_to_all(
            gate_part.astype(jnp.bfloat16), ("seq", "hid"), split_axis=0, concat_axis=1, tiled=True
        ).astype(gate_part.dtype),
        lax.all_to_all(
            up_part.astype(jnp.bfloat16), ("seq", "hid"), split_axis=0, concat_axis=1, tiled=True
        ).astype(up_part.dtype),
        lax.all_to_all(
            down_part.astype(jnp.bfloat16), ("seq", "hid"), split_axis=0, concat_axis=1, tiled=True
        ).astype(down_part.dtype),
    )
    o_grad = fold_copies(o_back, block_total)
    head_pick = (lax.iota(jnp.int32, H) == head_id).astype(jnp.float32)
    gap_full = (head_pick[:, None] * gap_piece_grad[None, :]).reshape(model)
    first_grad, second_grad, group_grad, gap_grad = lax.psum(
        (first_part, second_part, group_part, gap_full), ("seq", "hid")
    )
    return (
        output,
        input_grad,
        first_grad,
        fold_copies(q_back, block_total),
        fold_copies(f_back, block_total),
        fold_copies(i_back, block_total),
        o_grad,
        group_grad,
        gap_grad,
        second_grad,
        fold_copies(gate_back, block_total),
        fold_copies(up_back, block_total),
        fold_copies(down_back, block_total),
    )


F32 = jnp.float32
BF = jnp.bfloat16
MESH = pl.DeviceIdType.MESH
DMA = pltpu.SemaphoreType.DMA
VMEM = pltpu.VMEM
PIECES = 3
PARTS = 4
CUTS = PIECES * PARTS
AHEAD = (4, 4, 4, 4, 4, 4)
PACE = (4, 8)
TIMES = ((4, 5), (-1, 1), (12, 4), (0, 2), (8, 1), (0, 8))
VSPEC = pl.BlockSpec(memory_space=pltpu.VMEM)
ASPEC = pl.BlockSpec(memory_space=pl.ANY)
SSPEC = pl.BlockSpec(memory_space=pltpu.SMEM)


def place():
    h = lax.axis_index("hid")
    return h, h // 4, lax.rem(h // 2, 2), lax.rem(h, 2)


def partners():
    h, z, y, x = place()
    column = [lax.rem(z + k, 4) * 4 + lax.rem(h, 4) for k in (1, 2, 3)]
    return column, h + 2 - 4 * y, h + 1 - 2 * x


def greet(chips, core=False):
    gate = pltpu.get_barrier_semaphore()
    for chip in chips:
        pl.semaphore_signal(gate, inc=1, device_id={"hid": chip}, device_id_type=MESH)
    if core:
        other = 1 - lax.axis_index("seq")
        pl.semaphore_signal(gate, inc=1, device_id={"seq": other}, device_id_type=MESH)
    pl.semaphore_wait(gate, len(chips) + int(core))


def to_chip(src, dst, send, recv, chip):
    return pltpu.make_async_remote_copy(
        src_ref=src,
        dst_ref=dst,
        send_sem=send,
        recv_sem=recv,
        device_id={"hid": chip},
        device_id_type=MESH,
    )


def to_core(src, dst, send, recv):
    return pltpu.make_async_remote_copy(
        src_ref=src,
        dst_ref=dst,
        send_sem=send,
        recv_sem=recv,
        device_id={"seq": 1 - lax.axis_index("seq")},
        device_id_type=MESH,
    )


def comm_params(collective_id):
    return pltpu.CompilerParams(
        collective_id=collective_id, has_side_effects=True, vmem_limit_bytes=62 << 20
    )


class Cuts:
    def cut(self, c):
        i, j = c // PARTS, c % PARTS
        rows, cols = self.ref.shape[3] // PIECES, self.ref.shape[4] // PARTS
        return pl.ds(i * rows, rows), pl.ds(j * cols, cols), j % 2


class Gather(Cuts):
    def __init__(self, ref, sems):
        self.ref = ref
        self.s1, self.s2, self.s3, self.r1, self.r2, self.r3 = sems

    def start(self, c):
        h, z, y, x = place()
        column, py, px = partners()
        a, b, j = self.cut(c)
        ref = self.ref.at[z, y, x, a, b]
        for k in range(3):
            to_chip(ref, ref, self.s1, self.r1.at[c], column[k]).start()

    def second(self, c):
        h, z, y, x = place()
        column, py, px = partners()
        a, b, j = self.cut(c)
        three = self.ref.at[0:3, y, x, a, b]
        to_chip(three, three, self.s1, self.r1.at[c], px).wait_recv()
        ref = self.ref.at[:, y, x, a, b]
        to_chip(ref, ref, self.s2, self.r2.at[c], py if j else px).start()

    def third(self, c):
        h, z, y, x = place()
        column, py, px = partners()
        a, b, j = self.cut(c)
        got = self.ref.at[:, y, x, a, b]
        to_chip(got, got, self.s2, self.r2.at[c], px).wait_recv()
        ref = self.ref.at[:, :, x, a, b] if j else self.ref.at[:, y, :, a, b]
        to_chip(ref, ref, self.s3, self.r3, px if j else py).start()

    def finish(self):
        h, z, y, x = place()
        half, quarter, three = self.ref.at[:, 0], self.ref.at[:, 0, 0], self.ref.at[0:3, 0, 0]
        to_chip(half, half, self.s3, self.r3, x).wait_recv()
        for ref, sem in ((three, self.s1), (quarter, self.s2), (half, self.s3)):
            to_chip(ref, ref, sem, self.r3, x).wait_send()


def gather_sems():
    return [DMA, DMA, DMA, DMA((CUTS,)), DMA((CUTS,)), DMA]


class Scatter(Cuts):
    def __init__(self, ref, bufs, sems):
        self.ref, self.bufs = ref, bufs
        self.s1, self.s2, self.s3, self.r1, self.r2, self.r3 = sems

    def start(self, c):
        h, z, y, x = place()
        column, py, px = partners()
        a, b, j = self.cut(c)
        src = self.ref.at[:, :, 1 - x, a, b] if j else self.ref.at[:, 1 - y, :, a, b]
        to_chip(src, self.bufs[0].at[c], self.s1, self.r1.at[c], px if j else py).start()

    def second(self, c):
        h, z, y, x = place()
        column, py, px = partners()
        b1, t1, b2 = self.bufs[:3]
        a, b, j = self.cut(c)
        q = y if j else x
        to_chip(b1.at[c], b1.at[c], self.s1, self.r1.at[c], px).wait_recv()
        theirs = self.ref[:, 1 - q, x, a, b] if j else self.ref[:, y, 1 - q, a, b]
        b1[c, :, 1 - q] = (theirs.astype(F32) + b1[c, :, 1 - q].astype(F32)).astype(BF)
        to_chip(b1.at[c, :, 1 - q], b2.at[c], self.s2, self.r2.at[c], py if j else px).start()
        mine = self.ref[:, q, x, a, b] if j else self.ref[:, y, q, a, b]
        t1[c] = mine.astype(F32) + b1[c, :, q].astype(F32)

    def third(self, c):
        h, z, y, x = place()
        column, py, px = partners()
        b1, t1, b2, t2, b3 = self.bufs
        to_chip(b2.at[c], b2.at[c], self.s2, self.r2.at[c], px).wait_recv()
        t2[c] = t1[c, z] + b2[c, z].astype(F32)
        b2[c] = (t1[c] + b2[c].astype(F32)).astype(BF)
        for k in range(3):
            to_chip(
                b2.at[c, lax.rem(z + k + 1, 4)], b3.at[c, k], self.s3, self.r3.at[c], column[k]
            ).start()

    def last(self, c):
        h, z, y, x = place()
        b3, t2 = self.bufs[4], self.bufs[3]
        to_chip(b3.at[c], b3.at[c], self.s3, self.r3.at[c], x).wait_recv()
        return t2[c] + b3[c, 0].astype(F32) + b3[c, 1].astype(F32) + b3[c, 2].astype(F32)

    def finish(self):
        h, z, y, x = place()
        whole = self.bufs[0].at[:], self.bufs[2].at[:], self.bufs[4].at[:]
        for ref, sem in zip(whole, (self.s1, self.s2, self.s3)):
            to_chip(ref, ref, sem, self.r1.at[0], x).wait_send()


def scatter_bufs(rows, cols):
    n, r, w = CUTS, rows // PIECES, cols // PARTS
    return [
        VMEM((n, 4, 2, r, w), BF),
        VMEM((n, 4, r, w), F32),
        VMEM((n, 4, r, w), BF),
        VMEM((n, r, w), F32),
        VMEM((n, 3, r, w), BF),
    ]


def scatter_sems():
    return [DMA, DMA, DMA, DMA((CUTS,)), DMA((CUTS,)), DMA((CUTS,))]


def all_chips():
    h = lax.axis_index("hid")
    return [lax.rem(h + k, H) for k in range(1, H)]


class Plan:
    def __init__(self, *entries):
        self.entries = [[list(jobs), start, pace] for jobs, start, pace in entries]

    def step(self, t):
        for entry in self.entries:
            jobs, start, pace = entry
            if t >= start:
                for job in jobs[:pace]:
                    job()
                entry[0] = jobs[pace:]

    def rest(self):
        for entry in self.entries:
            for job in entry[0]:
                job()
            entry[0] = []

    def left(self, n):
        jobs, self.entries[n][0] = self.entries[n][0], []
        return jobs

    def during(self, jobs):
        for t, job in enumerate(jobs):
            job()
            self.step(t)


def unit_span(tiles, h):
    first = (tiles * h) // H
    return first, (tiles * (h + 1)) // H - first


def lanes(tile, count):
    return pl.ds(pl.multiple_of(tile * 128, 128), count * 128)


class Bulk:
    def __init__(self, items, tiles, depth, sems):
        self.items, self.tiles, self.depth = items, tiles, depth
        self.ss, self.rs, self.ls, self.xs, self.xr = sems
        self.least = tiles // H

    def sized(self, n, chip, act):
        if not self.items[n][3]:
            act(chip, 1)
            return
        first, count = unit_span(self.tiles, chip)
        if self.tiles % H == 0:
            act(first, self.least)
            return
        for number in (self.least, self.least + 1):
            pl.when(count == number)(functools.partial(act, first, number))

    def ours(self, view):
        half = H * self.depth
        return pl.ds(pl.multiple_of(view * half, half), half)

    def row(self, core, chip):
        return pl.ds(pl.multiple_of((core * H + chip) * self.depth, self.depth), self.depth)


class Fetch(Bulk):
    def copy(self, n, k, chip, first, count):
        h, b = lax.axis_index("hid"), lax.axis_index("seq")
        src, dst, at, _ = self.items[n]
        return to_chip(
            src.at[:, lanes(first, count)],
            dst.at[self.row(b, h), lanes(at, count)],
            self.ss.at[n],
            self.rs.at[n],
            chip,
        )

    def own(self, n, first, count):
        h, b = lax.axis_index("hid"), lax.axis_index("seq")
        src, dst, at, _ = self.items[n]
        return pltpu.make_async_copy(
            src.at[:, lanes(first, count)], dst.at[self.row(b, h), lanes(at, count)], self.ls.at[n]
        )

    def job(self, n, k):
        def run():
            chip = lax.rem(lax.axis_index("hid") + k, H)
            self.sized(
                n, chip, lambda first, count: self.copy(n, k, chip, first, count).start()
            )

        return run

    def jobs(self):
        return [self.job(n, k) for n in range(len(self.items)) for k in range(1, H)]

    def start_own(self):
        h = lax.axis_index("hid")
        for n, (_, dst, _, split) in enumerate(self.items):
            self.sized(n, h, lambda first, count: self.own(n, first, count).start())
            if split and self.tiles % H:

                @pl.when(unit_span(self.tiles, h)[1] == self.least)
                def _():
                    dst[:, self.least * 128 :] = jnp.zeros((dst.shape[0], 128), BF)

    def swap(self, n, tile, count, slot):
        b = lax.axis_index("seq")
        view = self.items[n][1].at[self.ours(b), lanes(tile, count)]
        return to_core(view, view, self.xs.at[n, slot], self.xr.at[n, slot])

    def each_swap(self, n, act):
        at, split = self.items[n][2:]
        act(self.swap(n, at, self.least if split else 1, 0))
        if split and self.tiles % H:

            @pl.when(unit_span(self.tiles, lax.axis_index("hid"))[1] > self.least)
            def _():
                act(self.swap(n, self.least, 1, 1))

    def arrive(self, n):
        h = lax.axis_index("hid")
        self.sized(n, h, lambda first, count: self.own(n, first, count).wait())
        self.sized(n, h, lambda first, count: self.rest(n, count).wait_recv())
        self.each_swap(n, lambda copy: copy.start())

    def settle(self, ns):
        for n in ns:
            self.each_swap(n, lambda copy: copy.wait())

    def finish(self):
        h = lax.axis_index("hid")
        for n in range(len(self.items)):
            self.sized(n, h, lambda first, count: self.rest(n, count).wait_send())

    def rest(self, n, count):
        src, dst, at, split = self.items[n]
        others = self.tiles - count if split else H - 1
        return to_chip(
            src.at[:, lanes(0, others)],
            dst.at[pl.ds(0, (H - 1) * self.depth), lanes(at, count)],
            self.ss.at[n],
            self.rs.at[n],
            lax.axis_index("hid"),
        )


class Return(Bulk):
    def __init__(self, items, parts, tiles, depth, sems):
        super().__init__(items, tiles, depth, sems)
        self.parts = parts

    def swap(self, p):
        part, total, _ = self.parts[p]
        return to_core(
            part.at[self.ours(1 - lax.axis_index("seq"))], total, self.xs.at[p, 0], self.xr.at[p, 0]
        )

    def add(self, p):
        def run():
            part, total, _ = self.parts[p]
            b = lax.axis_index("seq")
            self.swap(p).wait()
            half, step = total.shape[0], 128

            @pl.loop(0, half // step)
            def _(t):
                at = pl.ds(pl.multiple_of(t * step, step), step)
                own = pl.ds(pl.multiple_of(b * half + t * step, step), step)
                total[at] = (total[at].astype(F32) + part[own].astype(F32)).astype(BF)

            for n in self.parts[p][2]:
                h = lax.axis_index("hid")
                self.sized(n, h, lambda first, count: self.own(n, first, count).start())

        return run

    def copy(self, n, k, chip, first, count):
        dst, src, at, _ = self.items[n]
        return to_chip(
            src.at[self.row(0, chip), lanes(at, count)],
            dst.at[:, lanes(first, count)],
            self.ss.at[n],
            self.rs.at[n],
            chip,
        )

    def own(self, n, first, count):
        dst, src, at, _ = self.items[n]
        return pltpu.make_async_copy(
            src.at[self.row(0, lax.axis_index("hid")), lanes(at, count)],
            dst.at[:, lanes(first, count)],
            self.ls.at[n],
        )

    def job(self, n, k):
        def run():
            h = lax.axis_index("hid")
            chip = lax.rem(h + k, H)
            self.sized(n, h, lambda first, count: self.copy(n, k, chip, first, count).start())

        return run

    def jobs(self, p):
        return [self.add(p)] + [self.job(n, k) for n in self.parts[p][2] for k in range(1, H)]

    def finish(self):
        h = lax.axis_index("hid")
        for n in range(len(self.items)):
            self.sized(n, h, lambda first, count: self.own(n, first, count).wait())
            self.sized(n, h, lambda first, count: self.rest(n, count).wait())

    def rest(self, n, count):
        dst, src, at, split = self.items[n]
        others = self.tiles - count if split else H - 1
        return to_chip(
            src.at[pl.ds(0, (H - 1) * self.depth), lanes(at, count)],
            dst.at[:, lanes(0, others)],
            self.ss.at[n],
            self.rs.at[n],
            lax.axis_index("hid"),
        )


def bulk_sems(n):
    return [DMA((n,)), DMA((n,)), DMA((n,)), DMA((n, 2)), DMA((n, 2))]


def split_refs(refs, *counts):
    groups, at = [], 0
    for count in counts:
        groups.append(refs[at : at + count])
        at += count
    assert at == len(refs)
    return groups


def row_norm(rows):
    return lax.rsqrt(jnp.mean(rows * rows, axis=-1, keepdims=True) + EPS)


def gather_jobs(gather, ahead):
    lag = PARTS

    def step(t):
        def run():
            if t == 0:
                for c in range(ahead):
                    gather.start(c)
            if t < CUTS:
                gather.second(t)
                if t + ahead < CUTS:
                    gather.start(t + ahead)
            if t >= lag:
                gather.third(t - lag)

        return run

    return [step(t) for t in range(CUTS + lag)]


def scatter_jobs(scatter, ahead, rows_done, meanwhile=()):
    lag, held = PARTS, []

    def step(t):
        def run():
            if t == 0:
                for c in range(ahead):
                    scatter.start(c)
                for job in meanwhile:
                    job()
            if t < CUTS:
                scatter.second(t)
                if t + ahead < CUTS:
                    scatter.start(t + ahead)
            if 0 <= t - lag // 2 < CUTS:
                scatter.third(t - lag // 2)
            c = t - lag - lag // 2
            if c >= 0:
                held.append(scatter.last(c))
                if len(held) == PARTS:
                    rows_done(c // PARTS, jnp.concatenate(held, axis=1))
                    held.clear()

        return run

    return [step(t) for t in range(CUTS + lag + lag // 2)]


def turn_jobs(scatter, gather, ahead, rows_done, meanwhile=()):
    lag = PARTS

    def write(i, rows):
        rows_done(i, rows)
        if i == PIECES - 1:
            scatter.finish()
        for c in range(i * PARTS, (i + 1) * PARTS):
            gather.start(c)

    first = scatter_jobs(scatter, ahead, write, meanwhile)

    def step(t):
        def run():
            if t < len(first):
                first[t]()
            c = t - 2 * lag - lag // 2 - (PARTS - 1)
            if 0 <= c < CUTS:
                gather.second(c)
            if 0 <= c - lag < CUTS:
                gather.third(c - lag)

        return run

    return [step(t) for t in range(CUTS + 3 * lag + lag // 2 + PARTS - 1)]


def norm_back(rows, grad, gain):
    factor = row_norm(rows)
    normal = rows * factor
    scaled = grad * gain
    back = factor * (scaled - normal * jnp.mean(scaled * normal, axis=-1, keepdims=True))
    return back, jnp.sum(grad * normal, axis=0, keepdims=True)


def row_blocks(ref):
    size = 2 * ref.shape[1] * ref.shape[2] * ref.shape[3]
    return [(pl.ds(2 * n, 2), pl.ds(n * size, size)) for n in range(ref.shape[0] // 2)]


def merged(rows):
    return rows.reshape(-1, rows.shape[-1])


def doc_tile(lengths_ref, start, shape, dim):
    positions = start + lax.broadcasted_iota(jnp.int32, shape, dim)
    documents = jnp.full(shape, -1, jnp.int32)
    begin = jnp.int32(0)
    for n in range(lengths_ref.shape[0]):
        documents = documents + jnp.where(positions >= begin, 1, 0)
        begin = begin + lengths_ref[n]
    return documents


def layer_kernel(tiles, *refs):
    (
        (x_ref, c_ref, lengths, first_gain, second_gain, gain_ref, gap_all),
        weights,
        (out, in_grad, totals, *homes),
        (first, cot, second, mix, part, glu_part),
        (wqfi, wo, wg, wu, wd),
        (entry, middle, mid, dcol, drow, gap_ref),
        (lin, mixed, states, head, cum, d_head, d_lin, d_mixed, backs),
        (hidden, gate_low, up_low),
        (gqfi, go, gg, gu, gd),
        (tqfi, to, tg, tu, td),
        main_bufs,
        glu_bufs,
        gather_sets,
        scatter_sets,
        (f_out, f_in, b_out, b_in, fs, fr, bs, br, ls),
        (mine, theirs, chips, vs, vr, ws, wr),
        bulk_sets,
    ) = split_refs(refs, 7, 7, 10, 6, 5, 6, 9, 3, 5, 5, 5, 5, 24, 24, 9, 7, 20)
    q, f, i, o, g, u, d = weights
    hq, hf, hi, ho, hg, hu, hd = homes
    h, z, y, x = place()
    core = lax.axis_index("seq")
    depth, size = q.shape[0], x_ref.shape[1] // PIECES
    extent = lin.shape[0]
    mixer_in = Fetch(
        [(q, wqfi, 0, False), (f, wqfi, 1, False), (i, wqfi, 2, False), (o, wo, 0, False)],
        H,
        depth,
        bulk_sets[0:5],
    )
    units_in = Fetch(
        [(g, wg, 0, True), (u, wu, 0, True), (d, wd, 0, True)], tiles, depth, bulk_sets[5:10]
    )
    units_out = Return(
        [(hd, td, 0, True), (hg, tg, 0, True), (hu, tu, 0, True)],
        [(gd, td, (0,)), (gg, tg, (1,)), (gu, tu, (2,))],
        tiles,
        depth,
        bulk_sets[10:15],
    )
    mixer_out = Return(
        [(ho, to, 0, False), (hq, tqfi, 0, False), (hf, tqfi, 1, False), (hi, tqfi, 2, False)],
        [(go, to, (0,)), (gqfi, tqfi, (1, 2, 3))],
        H,
        depth,
        bulk_sets[15:20],
    )
    gathers = [
        Gather(ref, gather_sets[6 * n : 6 * n + 6])
        for n, ref in enumerate((first, cot, second, mix))
    ]
    scatters = [
        Scatter(ref, bufs, scatter_sets[6 * n : 6 * n + 6])
        for n, (ref, bufs) in enumerate(
            ((part, main_bufs), (part, main_bufs), (part, main_bufs), (glu_part, glu_bufs))
        )
    ]

    own = pltpu.make_async_copy(c_ref.at[0], cot.at[z, y, x], ls)
    own.start()
    mixer_in.start_own()
    for n in range(PIECES):
        at = pl.ds(n * size, size)
        rows = x_ref[0, at].astype(F32)
        entry[at] = rows
        first[z, y, x, at] = (rows * row_norm(rows) * first_gain[...]).astype(BF)
    greet(all_chips(), core=True)
    own.wait()

    def documents():
        gap_ref[...] = gap_all[pl.ds(h, 1)]
        base = core * extent
        for c, at in spans(extent):
            dcol[at] = doc_tile(lengths, base + c * SPAN, (SPAN, SPAN), 0)
            drow[8 * c : 8 * c + 8] = doc_tile(lengths, base + c * SPAN, (8, SPAN), 1)
        drow[8 * len(spans(extent)) :] = doc_tile(lengths, base - 1, (8, SPAN), 0)
        mine[...] = jnp.zeros_like(mine)
        units_in.start_own()

    mixer_jobs = mixer_in.jobs()
    plan = Plan(([documents], 0, 1), (mixer_jobs[: 3 * (H - 1)], *TIMES[0]))
    plan.during(gather_jobs(gathers[0], AHEAD[0]))
    plan.rest()
    for job in mixer_jobs[3 * (H - 1) :]:
        job()
    for n in range(3):
        mixer_in.arrive(n)
    gathers[0].finish()
    mixer_in.settle((0, 1, 2))
    plan = Plan((gather_jobs(gathers[1], AHEAD[1]), *TIMES[1]), (units_in.jobs(), *TIMES[2]))

    for n, at in row_blocks(first):
        lin[at] = jnp.dot(merged(first[n]), wqfi[...], preferred_element_type=F32)
        plan.step(-1)
    blocks = (lin, gap_ref, gain_ref, dcol, drow)
    mix_forward(blocks, mixed, states, head, cum, (f_out, f_in, fs, fr), lambda: plan.step(-1))
    mixer_in.arrive(3)
    mixer_in.settle((3,))
    for n, at in row_blocks(part):
        part[n] = times_t(head[at], wo[...]).astype(BF).reshape((2,) + part.shape[1:])
        plan.step(-1)

    def middle_rows(n, total):
        at = pl.ds(n * size, size)
        rows = entry[at] + total
        middle[at] = rows
        second[z, y, x, at] = (rows * row_norm(rows) * second_gain[...]).astype(BF)

    plan.during(turn_jobs(scatters[0], gathers[2], AHEAD[2], middle_rows))
    plan.rest()
    for n in range(3):
        units_in.arrive(n)
    gathers[1].finish()
    gathers[2].finish()
    mixer_in.finish()
    units_in.settle((0, 1, 2))
    units_in.finish()

    for n, at in row_blocks(second):
        rows = merged(second[n])
        gate_lin = jnp.dot(rows, wg[...], preferred_element_type=F32)
        up_lin = jnp.dot(rows, wu[...], preferred_element_type=F32)
        d_hidden = jnp.dot(merged(cot[n]), wd[...], preferred_element_type=F32)
        s = jax.nn.sigmoid(gate_lin)
        silu = gate_lin * s
        hidden[at] = (silu * up_lin).astype(BF)
        gate_low[at] = (d_hidden * up_lin * s * (1.0 + gate_lin * (1.0 - s))).astype(BF)
        up_low[at] = (d_hidden * silu).astype(BF)
        total = times_t(gate_low[at], wg[...]) + times_t(up_low[at], wu[...])
        part[n] = total.astype(BF).reshape((2,) + part.shape[1:])

    def grad_rows(n, total):
        at = pl.ds(n * size, size)
        back, gains = norm_back(middle[at], total, second_gain[...])
        mine[16:32] = mine[16:32] + gains.reshape(16, 128)
        rows = c_ref[0, at].astype(F32) + back
        mid[at] = rows
        mix[z, y, x, at] = rows.astype(BF)

    def out_rows(n, total):
        at = pl.ds(n * size, size)
        out[0, at] = (middle[at] + total).astype(BF)

    def outer(dst, rows, cols, giver, p):
        width = 512

        def piece(start):
            def run():
                at = pl.ds(start, width)
                dst[at] = outer_sum(merged(rows[:, :, :, :, at]), cols[...]).astype(BF)

            return run

        return [piece(start) for start in range(0, rows.shape[4], width)] + [
            lambda: giver.swap(p).start()
        ]

    def glu_block(n, at):
        def run():
            rows = times_t(hidden[at], wd[...]).astype(BF)
            glu_part[n] = rows.reshape((2,) + glu_part.shape[1:])

        return run

    returns = outer(gg, second, gate_low, units_out, 1) + units_out.jobs(0)
    returns += outer(gu, second, up_low, units_out, 2) + units_out.jobs(1) + units_out.jobs(2)
    outward = [glu_block(n, at) for n, at in row_blocks(glu_part)]
    outward += scatter_jobs(scatters[3], AHEAD[4], out_rows)
    plan = Plan((returns, *TIMES[3]), (outward, *TIMES[4]))
    plan.during(
        turn_jobs(
            scatters[1], gathers[3], AHEAD[3], grad_rows, outer(gd, cot, hidden, units_out, 0)
        )
    )
    gathers[3].finish()

    kept = plan.left(0), plan.left(1)
    plan = Plan((outer(go, mix, head, mixer_out, 0), 0, 2), (kept[0], 0, PACE[0]), (kept[1], 0, 1))
    for n, at in row_blocks(mix):
        d_head[at] = jnp.dot(merged(mix[n]), wo[...], preferred_element_type=F32)
        plan.step(0)
    group, gap = mix_backward(
        blocks, mixed, states, cum, d_head, d_lin, d_mixed, backs, (b_out, b_in, bs, br),
        lambda: plan.step(0),
    )
    mine[32:33] = group
    mine[40:41] = gap
    for n, at in row_blocks(part):
        part[n] = times_t(d_lin[at], wqfi[...]).astype(BF).reshape((2,) + part.shape[1:])

    def in_rows(n, total):
        at = pl.ds(n * size, size)
        back, gains = norm_back(entry[at], total, first_gain[...])
        in_grad[0, at] = mid[at] + back
        mine[0:16] = mine[0:16] + gains.reshape(16, 128)
        if n == PIECES - 1:
            swap = to_core(mine, theirs, vs, vr)
            swap.start()
            swap.wait()
            chips[h] = mine[...] + theirs[...]
            for k in range(1, H):
                to_chip(chips.at[h], chips.at[h], ws, wr, lax.rem(h + k, H)).start()

    for job in plan.left(0):
        job()
    kept = plan.left(1), plan.left(2)
    plan = Plan(
        (kept[0], 0, PACE[1]), (mixer_out.jobs(0) + mixer_out.jobs(1), *TIMES[5]), (kept[1], 0, 1)
    )
    plan.during(
        scatter_jobs(
            scatters[2], AHEAD[5], in_rows, outer(gqfi, first, d_lin, mixer_out, 1)
        )
    )
    plan.rest()
    others = chips.at[0 : H - 1]
    to_chip(others, others, ws, wr, h).wait()
    acc = chips[0, 0:40]
    for chip in range(1, H):
        acc = acc + chips[chip, 0:40]
    totals[0:40] = acc
    for chip in range(H):
        totals[40 + chip : 41 + chip] = chips[chip, 40:41]
    scatters[2].finish()
    scatters[3].finish()
    units_out.finish()
    mixer_out.finish()


def layer(inputs, cotangent, lengths, first_gain, second_gain, group_gain, gap_log, weights):
    _, rows, cols = inputs.shape
    depth, units = weights[-1].shape
    extent, count = H * rows, 2 * H * depth
    tiles = units // 128
    wide = -(-tiles // H) * 128
    home = lambda width: jax.ShapeDtypeStruct((depth, width), BF)
    full = VMEM((4, 2, 2, rows, cols), BF)
    local = VMEM((rows, cols), F32)
    tile = VMEM((extent, SPAN), F32)
    square = VMEM((SPAN, SPAN), F32)
    squares = VMEM((extent // SPAN, SPAN, SPAN), F32)
    widths = (384, 128, wide, wide, wide)
    return pl.pallas_call(
        functools.partial(layer_kernel, tiles),
        out_shape=[
            jax.ShapeDtypeStruct((1, rows, cols), BF),
            jax.ShapeDtypeStruct((1, rows, cols), F32),
            jax.ShapeDtypeStruct((56, 128), F32),
        ]
        + [home(cols)] * 4
        + [home(units)] * 3,
        in_specs=[VSPEC] * 2 + [SSPEC] + [VSPEC] * 4 + [ASPEC] * 7,
        out_specs=[VSPEC] * 3 + [ASPEC] * 7,
        scratch_shapes=[full] * 6
        + [VMEM((count, width), BF) for width in widths]
        + [local, local, local, VMEM((extent, SPAN), jnp.int32)]
        + [VMEM((8 * (extent // SPAN) + 8, SPAN), jnp.int32), VMEM((1, SPAN), F32)]
        + [VMEM((extent, 384), F32), tile, squares, VMEM((extent, SPAN), BF), tile]
        + [tile, VMEM((extent, 384), BF), tile, squares]
        + [VMEM((extent, wide), BF)] * 3
        + [VMEM((count, width), BF) for width in widths]
        + [VMEM((count // 2, width), BF) for width in widths]
        + scatter_bufs(rows, cols)
        + scatter_bufs(rows, cols)
        + gather_sems() * 4
        + scatter_sems() * 4
        + [square] * 4
        + [DMA] * 5
        + [VMEM((48, 128), F32), VMEM((48, 128), F32), VMEM((H, 48, 128), F32)]
        + [DMA, DMA, DMA, DMA]
        + bulk_sems(4)
        + bulk_sems(3)
        + bulk_sems(3)
        + bulk_sems(4),
        compiler_params=comm_params(1),
    )(
        inputs,
        cotangent,
        lengths,
        first_gain[None],
        second_gain[None],
        group_gain[None],
        gap_log.reshape(H, SPAN),
        *weights,
    )


def mm(left, right, at_left, at_right):
    return lax.dot_general(
        left.astype(BF),
        right.astype(BF),
        (((at_left,), (at_right,)), ((), ())),
        preferred_element_type=F32,
    )


def tri_sum(rows, reverse=False):
    r = lax.broadcasted_iota(jnp.int32, (SPAN, SPAN), 0)
    c = lax.broadcasted_iota(jnp.int32, (SPAN, SPAN), 1)
    picked = jnp.where((r <= c) if reverse else (r >= c), 1.0, 0.0).astype(BF)
    high = rows.astype(BF)
    rest = rows - high.astype(F32)
    middle = rest.astype(BF)
    low = rest - middle.astype(F32)
    return mm(picked, high, 1, 0) + mm(picked, middle, 1, 0) + mm(picked, low, 1, 0)


def span_gates(lin_ref, gap_ref, at):
    q_lin, f_lin, values = lin_ref[at, 0:128], lin_ref[at, 128:256], lin_ref[at, 256:384]
    s = jax.nn.sigmoid(q_lin)
    key = jnp.exp(gap_ref[...]) * jax.nn.sigmoid(-f_lin)
    return q_lin, f_lin, values, s, key


def span_masks(dcol_ref, drow_ref, c, at):
    r = lax.broadcasted_iota(jnp.int32, (SPAN, SPAN), 0)
    k = lax.broadcasted_iota(jnp.int32, (SPAN, SPAN), 1)
    dcol, drow = dcol_ref[at], drow_ref[8 * c : 8 * c + 1]
    last = (c + 1) * SPAN - 1
    end = dcol_ref[last : last + 1]
    if c:
        before = dcol_ref[c * SPAN - 1 : c * SPAN]
    else:
        count = drow_ref.shape[0]
        before = drow_ref[count - 8 : count - 7]
    same = jnp.where(jnp.logical_and(dcol == drow, r >= k), 1.0, 0.0)
    carried = jnp.where(dcol == before, 1.0, 0.0)
    keep = jnp.where(dcol == end, 1.0, 0.0)
    whole = jnp.where(end == before, 1.0, 0.0)
    return same, carried, keep, whole


def spans(extent):
    return [(c, pl.ds(c * SPAN, SPAN)) for c in range(extent // SPAN)]


def mix_forward(blocks, mixed_ref, states_ref, head_ref, cum_ref, handover, between):
    out_ref, in_ref, send, recv = handover
    lin_ref, gap_ref, gain_ref, dcol_ref, drow_ref = blocks
    steps = spans(lin_ref.shape[0])
    state = jnp.zeros((SPAN, SPAN), F32)
    for c, at in steps:
        q_lin, f_lin, values, s, key = span_gates(lin_ref, gap_ref, at)
        same, carried, keep, whole = span_masks(dcol_ref, drow_ref, c, at)
        cum = tri_sum(jnp.log1p(-key))
        cum_ref[at] = cum
        end = cum[SPAN - 1 : SPAN]
        fresh = mm(values, jnp.exp(end - cum) * key * keep, 0, 0)
        states_ref[c] = fresh
        state = state * (jnp.exp(end) * whole) + fresh
    out_ref[...] = state
    copy = to_core(out_ref, in_ref, send, recv)
    copy.start()
    between()
    copy.wait()
    state = in_ref[...] * lax.axis_index("seq").astype(F32)
    for c, at in steps:
        q_lin, f_lin, values, s, key = span_gates(lin_ref, gap_ref, at)
        same, carried, keep, whole = span_masks(dcol_ref, drow_ref, c, at)
        cum = cum_ref[at]
        end = cum[SPAN - 1 : SPAN]
        fresh = states_ref[c]
        states_ref[c] = state
        decayed = q_lin * s * jnp.exp(cum)
        scores = mm(decayed, key * jnp.exp(-cum), 1, 1) * same
        mixed = mm(scores, values, 1, 0) + carried * mm(decayed, state, 1, 1)
        mixed_ref[at] = mixed
        head_ref[at] = (mixed * row_norm(mixed) * gain_ref[...]).astype(BF)
        state = state * (jnp.exp(end) * whole) + fresh
        if c % 2:
            between()


def mix_backward(
    blocks, mixed_ref, states_ref, cum_ref, dhead_ref, dlin_ref, do_ref, back_ref, handover, between
):
    out_ref, in_ref, send, recv = handover
    lin_ref, gap_ref, gain_ref, dcol_ref, drow_ref = blocks
    steps = spans(lin_ref.shape[0])
    group = jnp.zeros((1, SPAN), F32)
    adjoint = jnp.zeros((SPAN, SPAN), F32)
    for c, at in reversed(steps):
        d_mixed, gains = norm_back(mixed_ref[at], dhead_ref[at], gain_ref[...])
        group = group + gains
        do_ref[at] = d_mixed
        q_lin, f_lin, values, s, key = span_gates(lin_ref, gap_ref, at)
        same, carried, keep, whole = span_masks(dcol_ref, drow_ref, c, at)
        cum = cum_ref[at]
        back = mm(d_mixed, carried * (q_lin * s * jnp.exp(cum)), 0, 0)
        back_ref[c] = back
        adjoint = adjoint * (jnp.exp(cum[SPAN - 1 : SPAN]) * whole) + back
    out_ref[...] = adjoint
    copy = to_core(out_ref, in_ref, send, recv)
    copy.start()
    between()
    copy.wait()
    adjoint = in_ref[...] * (1 - lax.axis_index("seq")).astype(F32)
    gap = jnp.zeros((1, SPAN), F32)
    for c, at in reversed(steps):
        q_lin, f_lin, values, s, key = span_gates(lin_ref, gap_ref, at)
        same, carried, keep, whole = span_masks(dcol_ref, drow_ref, c, at)
        cum, d_mixed, state = cum_ref[at], do_ref[at], states_ref[c]
        grow, shrink = jnp.exp(-cum), jnp.exp(cum)
        end = cum[SPAN - 1 : SPAN]
        decayed, grown = q_lin * s * shrink, key * grow
        rest = jnp.exp(end - cum) * keep
        tail, through = rest * key, jnp.exp(end) * whole
        scores = mm(decayed, grown, 1, 1) * same
        d_scores = mm(d_mixed, values, 1, 1) * same
        d_values = mm(scores, d_mixed, 0, 0) + mm(tail, adjoint, 1, 1)
        d_decayed = mm(d_scores, grown, 1, 0) + carried * mm(d_mixed, state, 1, 0)
        d_grown = mm(d_scores, decayed, 0, 0)
        d_tail = mm(values, adjoint, 1, 0)
        held = tail * d_tail
        d_cum = decayed * d_decayed - grown * d_grown - held
        d_end = jnp.sum(held, axis=0, keepdims=True) + through * jnp.sum(
            state * adjoint, axis=0, keepdims=True
        )
        d_log = tri_sum(d_cum, reverse=True) + d_end
        d_key = d_grown * grow + d_tail * rest - d_log / (1.0 - key)
        scaled = d_key * key
        gap = gap + jnp.sum(scaled, axis=0, keepdims=True)
        dlin_ref[at, 0:128] = (d_decayed * shrink * s * (1.0 + q_lin * (1.0 - s))).astype(BF)
        dlin_ref[at, 128:256] = (-scaled * jax.nn.sigmoid(f_lin)).astype(BF)
        dlin_ref[at, 256:384] = d_values.astype(BF)
        adjoint = adjoint * through + back_ref[c]
        if c % 2:
            between()
    return group, gap


def fast_body(
    inputs,
    cotangent,
    lengths,
    first_gain,
    q_weight,
    f_weight,
    i_weight,
    o_weight,
    group_gain,
    gap_log,
    second_gain,
    gate_weight,
    up_weight,
    down_weight,
):
    model = inputs.shape[2]
    output, input_grad, totals, *grads = layer(
        inputs,
        cotangent,
        lengths,
        first_gain,
        second_gain,
        group_gain,
        gap_log,
        (q_weight, f_weight, i_weight, o_weight, gate_weight, up_weight, down_weight),
    )
    q_grad, f_grad, i_grad, o_grad, gate_grad, up_grad, down_grad = (
        grad.astype(F32) for grad in grads
    )
    return (
        output,
        input_grad,
        totals[0:16].reshape(model),
        q_grad,
        f_grad,
        i_grad,
        o_grad,
        totals[32],
        totals[40:56].reshape(model),
        totals[16:32].reshape(model),
        gate_grad,
        up_grad,
        down_grad,
    )


def solution(mesh):
    placed = (
        P("seq", "hid", None),
        P("seq", "hid", None),
        P(),
        P(),
        P(("seq", "hid"), None),
        P(("seq", "hid"), None),
        P(("seq", "hid"), None),
        P(("seq", "hid"), None),
        P(),
        P(),
        P(),
        P(("seq", "hid"), None),
        P(("seq", "hid"), None),
        P(("seq", "hid"), None),
    )
    body = fast_body if mesh.shape["hid"] == H else wide_body
    return jax.shard_map(
        body,
        mesh=mesh,
        in_specs=placed,
        out_specs=(
            P("seq", "hid", None),
            P("seq", "hid", None),
            P(),
            P(("seq", "hid"), None),
            P(("seq", "hid"), None),
            P(("seq", "hid"), None),
            P(("seq", "hid"), None),
            P(),
            P(),
            P(),
            P(("seq", "hid"), None),
            P(("seq", "hid"), None),
            P(("seq", "hid"), None),
        ),
        check_vma=False,
    )
```

profile of v0, /device:TPU:2, one launch (start us, length us, event | category | flops | bytes accessed | tf_op | source)
XLA Modules:
  0.0 389.8 jit_solution(14847048349317150157)
XLA Ops:
  0.7 376.9 %shard_map.237 = (bf16[1,48,2048]{2,1,0:T(8,128)(2,1)}, f32[1,48,2048]{2,1,0:T(8,128)}, f32[56,128]{1,0:T(8,128)}, bf16[64,2048]{1,0:T(8,128)(2,1)}, bf16[64,204...) custom-call(bf16[1,48,2048]{2,1,0:T(8,128)(2,1)} %refs_0_.1, ...), custom_call_target="tpu_custom_call" | custom-call | tf_op jit(solution)/shard_map/pallas_call | solution.py:1177
  377.6 0.0 copy-start.1
  377.6 1.4 slice_bitcast_fusion
  379.0 1.2 slice_bitcast_fusion.3
  380.2 2.3 convert_element_type.25
  382.5 0.0 copy-start
  382.5 0.0 copy-done.1
  382.5 1.2 convert_element_type.26
  383.7 0.0 copy-start.6
  383.7 0.1 copy-done
  383.8 0.0 copy-start.5
  383.8 0.0 copy-start.4
  383.8 1.2 convert_element_type.27
  385.0 0.0 copy-start.3
  385.0 0.0 copy-done.6
  385.0 0.0 copy-start.7
  385.0 0.8 convert_element_type.21
  385.9 0.0 copy-start.2
  385.9 0.0 copy-done.5
  385.9 0.8 convert_element_type.22
  386.7 0.0 copy-done.4
  386.7 0.8 convert_element_type.23
  387.5 0.0 copy-done.3
  387.5 0.8 convert_element_type.24
  388.4 0.0 copy-done.7
  388.4 0.7 copy.29
  389.0 0.0 copy-done.2
  389.0 0.7 copy.30
Async XLA Ops:
  377.6 4.9 %copy-start.1 = (bf16[64,5632]{1,0:T(8,128)(2,1)S(1)}, bf16[64,5632]{1,0:T(8,128)(2,1)}, u32[]{:S(2)}) copy-start(bf16[64,5632]{1,0:T(8,128)(2,1)} %get-tuple-element.31) | copy-start | bytes 2162692
  382.5 1.3 copy-start
  383.7 1.4 copy-start.6
  383.8 2.0 copy-start.5
  383.8 2.9 copy-start.4
  385.0 2.5 copy-start.3
  385.0 3.3 copy-start.7
  385.9 3.2 copy-start.2
where the time goes:
time: 392 us; the launch traced here: 390 us
  Pallas kernels  377 us (96%)
  other arithmetic  8 us (2%)
  local copies, waits for them, and re-layouts  4.19 us (1%)
    pallas_call x1, Pallas kernels, layer(): pl.pallas_call(functools.partial(layer_kernel, tiles), out_shape=[jax.Sha...  377 us
    convert_element_type x7, other arithmetic, fast_body(): grad.astype(F32)  8 us

commit v1 on v0

--- a/solution.py
+++ b/solution.py
@@ -415,7 +415,7 @@
 CUTS = PIECES * PARTS
 AHEAD = (4, 4, 4, 4, 4, 4)
 PACE = (4, 8)
-TIMES = ((4, 5), (-1, 1), (12, 4), (0, 2), (8, 1), (0, 8))
+TIMES = ((4, 5), (-1, 1), (16, 6), (6, 2), (8, 1), (0, 8))
 VSPEC = pl.BlockSpec(memory_space=pltpu.VMEM)
 ASPEC = pl.BlockSpec(memory_space=pl.ANY)
 SSPEC = pl.BlockSpec(memory_space=pltpu.SMEM)
@@ -1219,13 +1219,23 @@
     )
 
 
+def product(left, right, at_left, at_right):
+    return lax.dot_general(
+        left, right, (((at_left,), (at_right,)), ((), ())), preferred_element_type=F32
+    )
+
+
+def halves(rows):
+    high = rows.astype(BF)
+    return high, (rows - high.astype(F32)).astype(BF)
+
+
 def mm(left, right, at_left, at_right):
-    return lax.dot_general(
-        left.astype(BF),
-        right.astype(BF),
-        (((at_left,), (at_right,)), ((), ())),
-        preferred_element_type=F32,
-    )
+    left_high, left_low = halves(left)
+    right_high, right_low = halves(right)
+    small = product(left_high, right_low, at_left, at_right)
+    small = small + product(left_low, right_high, at_left, at_right)
+    return product(left_high, right_high, at_left, at_right) + small
 
 
 def tri_sum(rows, reverse=False):
@@ -1234,9 +1244,8 @@
     picked = jnp.where((r <= c) if reverse else (r >= c), 1.0, 0.0).astype(BF)
     high = rows.astype(BF)
     rest = rows - high.astype(F32)
-    middle = rest.astype(BF)
-    low = rest - middle.astype(F32)
-    return mm(picked, high, 1, 0) + mm(picked, middle, 1, 0) + mm(picked, low, 1, 0)
+    middle, low = halves(rest)
+    return product(picked, high, 1, 0) + product(picked, middle, 1, 0) + product(picked, low, 1, 0)
 
 
 def span_gates(lin_ref, gap_ref, at):
@@ -1363,6 +1372,45 @@
     return group, gap
 
 
+def finish_kernel(out_ref, in_ref, totals_ref, *refs):
+    out, in_grad, first, second, group, gap = refs[7:13]
+    out[...] = out_ref[...]
+    in_grad[...] = in_ref[...]
+    first[...] = totals_ref[0:16]
+    second[...] = totals_ref[16:32]
+    group[...] = totals_ref[32:33]
+    gap[...] = totals_ref[40:56]
+    for src, dst in zip(refs[:7], refs[13:]):
+        dst[...] = src[...].astype(F32)
+
+
+def finish(output, input_grad, totals, grads):
+    depth = grads[0].shape[0]
+    rows, cols = output.shape[1:]
+    steps = 4
+    piece = depth // steps
+    local = pl.BlockSpec((1, piece, cols), lambda n: (0, jnp.minimum(n, rows // piece - 1), 0))
+    whole = lambda height: pl.BlockSpec((height, 128), lambda n: (0, 0))
+    grad = [pl.BlockSpec((piece, g.shape[1]), lambda n: (n, 0)) for g in grads]
+    vector = lambda height: jax.ShapeDtypeStruct((height, 128), F32)
+    return pl.pallas_call(
+        finish_kernel,
+        grid=(steps,),
+        out_shape=[
+            jax.ShapeDtypeStruct(output.shape, BF),
+            jax.ShapeDtypeStruct(input_grad.shape, F32),
+            vector(16),
+            vector(16),
+            vector(1),
+            vector(16),
+        ]
+        + [jax.ShapeDtypeStruct(g.shape, F32) for g in grads],
+        in_specs=[local, local, whole(56)] + grad,
+        out_specs=[local, local, whole(16), whole(16), whole(1), whole(16)] + grad,
+        compiler_params=pltpu.CompilerParams(vmem_limit_bytes=62 << 20),
+    )(output, input_grad, totals, *grads)
+
+
 def fast_body(
     inputs,
     cotangent,
@@ -1390,20 +1438,21 @@
         gap_log,
         (q_weight, f_weight, i_weight, o_weight, gate_weight, up_weight, down_weight),
     )
-    q_grad, f_grad, i_grad, o_grad, gate_grad, up_grad, down_grad = (
-        grad.astype(F32) for grad in grads
-    )
+    output, input_grad, first_grad, second_grad, group_grad, gap_grad, *grads = finish(
+        output, input_grad, totals, grads
+    )
+    q_grad, f_grad, i_grad, o_grad, gate_grad, up_grad, down_grad = grads
     return (
         output,
         input_grad,
-        totals[0:16].reshape(model),
+        first_grad.reshape(model),
         q_grad,
         f_grad,
         i_grad,
         o_grad,
-        totals[32],
-        totals[40:56].reshape(model),
-        totals[16:32].reshape(model),
+        group_grad.reshape(SPAN),
+        gap_grad.reshape(model),
+        second_grad.reshape(model),
         gate_grad,
         up_grad,
         down_grad,

time: 392 us -> 379 us (0.967)
  other arithmetic: 8 us -> 0 us
  local copies, waits for them, and re-layouts: 4.19 us -> 0 us
    convert_element_type x7 -> x0, other arithmetic: 8 us -> none  [fast_body(): grad.astype(F32)]
    pallas_call x1, Pallas kernels: 377 us -> 370 us  [layer(): pl.pallas_call(functools.partial(layer_kernel, tiles), out_shape=[jax.Sha...]
    pallas_call x0 -> x1, Pallas kernels: none -> 5.48 us  [finish(): pl.pallas_call(finish_kernel, grid=(steps,), out_shape=[jax.ShapeDtypeStr...]
where the time goes in v1:
time: 379 us; the launch traced here: 377 us
  Pallas kernels  376 us (99%)
    pallas_call x1, Pallas kernels, layer(): pl.pallas_call(functools.partial(layer_kernel, tiles), out_shape=[jax.Sha...  370 us

profile of v1, /device:TPU:2, one launch (start us, length us, event | category | flops | bytes accessed | tf_op | source)
XLA Modules:
  0.0 376.5 jit_solution(6870825961381928878)
XLA Ops:
  0.7 370.2 %shard_map.237 = (bf16[1,48,2048]{2,1,0:T(8,128)(2,1)}, f32[1,48,2048]{2,1,0:T(8,128)}, f32[56,128]{1,0:T(8,128)}, bf16[64,2048]{1,0:T(8,128)(2,1)}, bf16[64,204...) custom-call(bf16[1,48,2048]{2,1,0:T(8,128)(2,1)} %refs_0_.1, ...), custom_call_target="tpu_custom_call" | custom-call | tf_op jit(solution)/shard_map/pallas_call | solution.py:1177
  370.9 5.5 %shard_map.238 = (bf16[1,48,2048]{2,1,0:T(8,128)(2,1)}, f32[1,48,2048]{2,1,0:T(8,128)}, f32[16,128]{1,0:T(8,128)}, f32[16,128]{1,0:T(8,128)}, f32[1,128]{1,0:T(1...) custom-call(bf16[1,48,2048]{2,1,0:T(8,128)(2,1)} %get-tuple-element., ...), custom_call_target="tpu_custom_call" | custom-call | tf_op jit(solution)/shard_map/pallas_call | solution.py:1396

commit v2 on v1

--- a/solution.py
+++ b/solution.py
@@ -415,7 +415,7 @@
 CUTS = PIECES * PARTS
 AHEAD = (4, 4, 4, 4, 4, 4)
 PACE = (4, 8)
-TIMES = ((4, 5), (-1, 1), (16, 6), (6, 2), (8, 1), (0, 8))
+TIMES = ((4, 5), (-1, 1), (16, 6), (8, 2), (8, 1), (0, 8))
 VSPEC = pl.BlockSpec(memory_space=pltpu.VMEM)
 ASPEC = pl.BlockSpec(memory_space=pl.ANY)
 SSPEC = pl.BlockSpec(memory_space=pltpu.SMEM)
@@ -939,7 +939,7 @@
         (wqfi, wo, wg, wu, wd),
         (entry, middle, mid, dcol, drow, gap_ref),
         (lin, mixed, states, head, cum, d_head, d_lin, d_mixed, backs),
-        (hidden, gate_low, up_low),
+        (hidden, gate_low, up_low, gate_ref, up_ref),
         (gqfi, go, gg, gu, gd),
         (tqfi, to, tg, tu, td),
         main_bufs,
@@ -949,7 +949,7 @@
         (f_out, f_in, b_out, b_in, fs, fr, bs, br, ls),
         (mine, theirs, chips, vs, vr, ws, wr),
         bulk_sets,
-    ) = split_refs(refs, 7, 7, 10, 6, 5, 6, 9, 3, 5, 5, 5, 5, 24, 24, 9, 7, 20)
+    ) = split_refs(refs, 7, 7, 10, 6, 5, 6, 9, 5, 5, 5, 5, 5, 24, 24, 9, 7, 20)
     q, f, i, o, g, u, d = weights
     hq, hf, hi, ho, hg, hu, hd = homes
     h, z, y, x = place()
@@ -1042,18 +1042,22 @@
 
     plan.during(turn_jobs(scatters[0], gathers[2], AHEAD[2], middle_rows))
     plan.rest()
-    for n in range(3):
-        units_in.arrive(n)
-    gathers[1].finish()
+    units_in.arrive(0)
+    units_in.arrive(1)
     gathers[2].finish()
-    mixer_in.finish()
-    units_in.settle((0, 1, 2))
-    units_in.finish()
+    units_in.settle((0, 1))
 
     for n, at in row_blocks(second):
         rows = merged(second[n])
-        gate_lin = jnp.dot(rows, wg[...], preferred_element_type=F32)
-        up_lin = jnp.dot(rows, wu[...], preferred_element_type=F32)
+        gate_ref[at] = jnp.dot(rows, wg[...], preferred_element_type=F32)
+        up_ref[at] = jnp.dot(rows, wu[...], preferred_element_type=F32)
+    units_in.arrive(2)
+    gathers[1].finish()
+    mixer_in.finish()
+    units_in.settle((2,))
+    units_in.finish()
+    for n, at in row_blocks(cot):
+        gate_lin, up_lin = gate_ref[at], up_ref[at]
         d_hidden = jnp.dot(merged(cot[n]), wd[...], preferred_element_type=F32)
         s = jax.nn.sigmoid(gate_lin)
         silu = gate_lin * s
@@ -1192,6 +1196,7 @@
         + [VMEM((extent, 384), F32), tile, squares, VMEM((extent, SPAN), BF), tile]
         + [tile, VMEM((extent, 384), BF), tile, squares]
         + [VMEM((extent, wide), BF)] * 3
+        + [VMEM((extent, wide), F32)] * 2
         + [VMEM((count, width), BF) for width in widths]
         + [VMEM((count // 2, width), BF) for width in widths]
         + scatter_bufs(rows, cols)

time: 379 us -> 372 us (0.982)
  Pallas kernels: 376 us -> 369 us
    pallas_call x1, Pallas kernels: 370 us -> 364 us  [layer(): pl.pallas_call(functools.partial(layer_kernel, tiles), out_shape=[jax.Sha...]
where the time goes in v2:
time: 372 us; the launch traced here: 370 us
  Pallas kernels  369 us (99%)
    pallas_call x1, Pallas kernels, layer(): pl.pallas_call(functools.partial(layer_kernel, tiles), out_shape=[jax.Sha...  364 us

profile of v2, /device:TPU:2, one launch (start us, length us, event | category | flops | bytes accessed | tf_op | source)
XLA Modules:
  0.0 370.2 jit_solution(8192505046798598610)
XLA Ops:
  0.7 363.9 %shard_map.237 = (bf16[1,48,2048]{2,1,0:T(8,128)(2,1)}, f32[1,48,2048]{2,1,0:T(8,128)}, f32[56,128]{1,0:T(8,128)}, bf16[64,2048]{1,0:T(8,128)(2,1)}, bf16[64,204...) custom-call(bf16[1,48,2048]{2,1,0:T(8,128)(2,1)} %refs_0_.1, ...), custom_call_target="tpu_custom_call" | custom-call | tf_op jit(solution)/shard_map/pallas_call | solution.py:1181
  364.6 5.5 %shard_map.238 = (bf16[1,48,2048]{2,1,0:T(8,128)(2,1)}, f32[1,48,2048]{2,1,0:T(8,128)}, f32[16,128]{1,0:T(8,128)}, f32[16,128]{1,0:T(8,128)}, f32[1,128]{1,0:T(1...) custom-call(bf16[1,48,2048]{2,1,0:T(8,128)(2,1)} %get-tuple-element., ...), custom_call_target="tpu_custom_call" | custom-call | tf_op jit(solution)/shard_map/pallas_call | solution.py:1401

commit v3 on v2

--- a/solution.py
+++ b/solution.py
@@ -413,7 +413,7 @@
 PIECES = 3
 PARTS = 4
 CUTS = PIECES * PARTS
-AHEAD = (4, 4, 4, 4, 4, 4)
+AHEAD = (4, 4, 3, 3, 4, 4)
 PACE = (4, 8)
 TIMES = ((4, 5), (-1, 1), (16, 6), (8, 2), (8, 1), (0, 8))
 VSPEC = pl.BlockSpec(memory_space=pltpu.VMEM)

time: 372 us -> 371 us (level)
  no operation moved by 1% of the time
where the time goes in v3:
time: 371 us; the launch traced here: 368 us
  Pallas kernels  368 us (99%)
    pallas_call x1, Pallas kernels, layer(): pl.pallas_call(functools.partial(layer_kernel, tiles), out_shape=[jax.Sha...  362 us

profile of v3, /device:TPU:2, one launch (start us, length us, event | category | flops | bytes accessed | tf_op | source)
XLA Modules:
  0.0 368.4 jit_solution(6874064519324492205)
XLA Ops:
  0.7 362.1 %shard_map.237 = (bf16[1,48,2048]{2,1,0:T(8,128)(2,1)}, f32[1,48,2048]{2,1,0:T(8,128)}, f32[56,128]{1,0:T(8,128)}, bf16[64,2048]{1,0:T(8,128)(2,1)}, bf16[64,204...) custom-call(bf16[1,48,2048]{2,1,0:T(8,128)(2,1)} %refs_0_.1, ...), custom_call_target="tpu_custom_call" | custom-call | tf_op jit(solution)/shard_map/pallas_call | solution.py:1181
  362.7 5.5 %shard_map.238 = (bf16[1,48,2048]{2,1,0:T(8,128)(2,1)}, f32[1,48,2048]{2,1,0:T(8,128)}, f32[16,128]{1,0:T(8,128)}, f32[16,128]{1,0:T(8,128)}, f32[1,128]{1,0:T(1...) custom-call(bf16[1,48,2048]{2,1,0:T(8,128)(2,1)} %get-tuple-element., ...), custom_call_target="tpu_custom_call" | custom-call | tf_op jit(solution)/shard_map/pallas_call | solution.py:1401
